TPU v7x, 32 devices: a whole 2x2x4 slice. The times are simulated.
32 devices in a mesh: expert: 4 (over y, core), replica: 2 (over x), seq: 4 (over z).
Axes of the slice: x: 2, y: 2, z: 4, core: 2. Of those that a mesh axis runs over, the one named last changes fastest.
Arguments:
- tokens: bfloat16 [1536, 3584], P(('expert', 'replica'), 'seq'), may hold values from -6 to 6
- cotangent: bfloat16 [1536, 3584], P(('expert', 'replica'), 'seq'), may hold values from -6 to 6
- route_weight: float32 [1536], P(('expert', 'replica')), may hold values from 0.1 to 1
- expert_ids: int32 [1536, 1], P(('expert', 'replica')), may hold values from 0 to 3; in each aligned block of 192 rows (0 to 191, 192 to 383, ...) at most 72 rows name the same one
- gate_weight: bfloat16 [4, 3584, 1024], P('expert', 'seq', 'replica'), may hold values from -0.09375 to 0.09375
- up_weight: bfloat16 [4, 3584, 1024], P('expert', 'seq', 'replica'), may hold values from -0.09375 to 0.09375
- down_weight: bfloat16 [4, 1024, 3584], P('expert', 'replica', 'seq'), may hold values from -0.1875 to 0.1875
Outputs:
- token_grad: bfloat16 [1536, 3584], P(('expert', 'replica'), 'seq')
- gate_grad: bfloat16 [4, 3584, 1024], P('expert', 'seq', 'replica')
- up_grad: bfloat16 [4, 3584, 1024], P('expert', 'seq', 'replica')
- down_grad: bfloat16 [4, 1024, 3584], P('expert', 'replica', 'seq')
Inputs may be any that keep to these rules, and one draw needn't show every extreme that they name: `expert_ids`: among the 192 tokens of one block (the tokens of one device) no expert is named more than 72 times, a bound that some block reaches.
All inputs are finite; a program needn't handle non-finite values.
Results may differ from a plain program's by a relative error of at most 0.02.
Values may be sent and summed in bfloat16 or wider, within the bound.
No kernel may reach another device: no remote copies, remote signals or barrier semaphores. Data moves between devices by JAX's collectives and lax.ppermute only.
A program may use at most 64 MiB of HBM per device.

v0:
```python
import jax
import jax.numpy as jnp
from jax import lax
from jax.sharding import PartitionSpec as P


def matmul_last(left, right):
    return lax.dot_general(
        left, right, (((1,), (1,)), ((), ())), preferred_element_type=jnp.float32
    )


def matmul_first(left, right):
    return lax.dot_general(
        left, right, (((0,), (0,)), ((), ())), preferred_element_type=jnp.float32
    )


def local(tokens, cotangent, route_weight, expert_ids, gate_weight, up_weight, down_weight):
    n_expert = lax.axis_size("expert")
    count = tokens.shape[0]
    quarter = tokens.shape[1]
    capacity = 3 * count // (2 * n_expert)
    chosen = expert_ids[:, 0]
    onehot = (chosen[:, None] == jnp.arange(n_expert, dtype=jnp.int32)[None, :]).astype(jnp.int32)
    before = jnp.cumsum(onehot, axis=0) - onehot
    within = jnp.sum(before * onehot, axis=1)
    target = chosen * capacity + within
    table = (
        jnp.full((n_expert * capacity,), count, jnp.int32)
        .at[target]
        .set(jnp.arange(count, dtype=jnp.int32))
    )
    blank = jnp.zeros((1, quarter), jnp.bfloat16)
    padded_x = jnp.concatenate([tokens, blank], axis=0)
    scaled = (route_weight[:, None] * cotangent.astype(jnp.float32)).astype(jnp.bfloat16)
    padded_g = jnp.concatenate([scaled, blank], axis=0)
    send_x = padded_x[table].reshape(n_expert, capacity, quarter)
    send_g = padded_g[table].reshape(n_expert, capacity, quarter)
    recv_x = lax.all_to_all(send_x, "expert", split_axis=0, concat_axis=0, tiled=True)
    rows_x = recv_x.reshape(-1, quarter)
    full_gate, full_up, full_down = (
        lax.all_gather(gate_weight, "replica", axis=2, tiled=True),
        lax.all_gather(up_weight, "replica", axis=2, tiled=True),
        lax.all_gather(down_weight, "replica", axis=1, tiled=True),
    )
    w_gate = full_gate[0]
    w_up = full_up[0]
    w_down = full_down[0]
    part_gate = jnp.dot(rows_x, w_gate, preferred_element_type=jnp.float32)
    part_up = jnp.dot(rows_x, w_up, preferred_element_type=jnp.float32)
    gate, upper = (
        lax.psum(part_gate.astype(jnp.bfloat16), "seq").astype(jnp.float32),
        lax.psum(part_up.astype(jnp.bfloat16), "seq").astype(jnp.float32),
    )
    sigma = jax.nn.sigmoid(gate)
    active = gate * sigma
    hidden = (active * upper).astype(jnp.bfloat16)
    recv_g = lax.all_to_all(send_g, "expert", split_axis=0, concat_axis=0, tiled=True)
    rows_g = recv_g.reshape(-1, quarter)
    part_dh = matmul_last(rows_g, w_down)
    hgrad = lax.psum(part_dh.astype(jnp.bfloat16), "seq").astype(jnp.float32)
    gate_delta = (hgrad * upper * sigma * (1.0 + gate * (1.0 - sigma))).astype(jnp.bfloat16)
    up_delta = (hgrad * active).astype(jnp.bfloat16)
    out_rows = (matmul_last(gate_delta, w_gate) + matmul_last(up_delta, w_up)).astype(jnp.bfloat16)
    returned = lax.all_to_all(
        out_rows.reshape(n_expert, capacity, quarter),
        "expert",
        split_axis=0,
        concat_axis=0,
        tiled=True,
    )
    returned = returned.reshape(-1, quarter)
    token_grad = (route_weight[:, None] * returned[target].astype(jnp.float32)).astype(jnp.bfloat16)
    grad_gate = matmul_first(rows_x, gate_delta).astype(jnp.bfloat16)[None]
    grad_up = matmul_first(rows_x, up_delta).astype(jnp.bfloat16)[None]
    grad_down = matmul_first(hidden, rows_g).astype(jnp.bfloat16)[None]
    pieces_gate, pieces_up = (
        lax.all_to_all(grad_gate, "replica", split_axis=2, concat_axis=0, tiled=True),
        lax.all_to_all(grad_up, "replica", split_axis=2, concat_axis=0, tiled=True),
    )
    pieces_down = lax.all_to_all(grad_down, "replica", split_axis=1, concat_axis=0, tiled=True)
    gate_grad = jnp.sum(pieces_gate.astype(jnp.float32), axis=0, keepdims=True).astype(jnp.bfloat16)
    up_grad = jnp.sum(pieces_up.astype(jnp.float32), axis=0, keepdims=True).astype(jnp.bfloat16)
    down_grad = jnp.sum(pieces_down.astype(jnp.float32), axis=0, keepdims=True).astype(jnp.bfloat16)
    return (token_grad, gate_grad, up_grad, down_grad)


def solution(mesh):
    placed = (
        P(("expert", "replica"), "seq"),
        P(("expert", "replica"), "seq"),
        P(("expert", "replica")),
        P(("expert", "replica"), None),
        P("expert", "seq", "replica"),
        P("expert", "seq", "replica"),
        P("expert", "replica", "seq"),
    )
    return jax.shard_map(
        local,
        mesh=mesh,
        in_specs=placed,
        out_specs=(
            P(("expert", "replica"), "seq"),
            P("expert", "seq", "replica"),
            P("expert", "seq", "replica"),
            P("expert", "replica", "seq"),
        ),
        check_vma=False,
    )
```

profile of v0, /device:TPU:0, one launch (start us, length us, event | category | flops | bytes accessed | tf_op | source)
XLA Modules:
  0.0 313.1 jit_solution(9565606176509443783)
XLA Ops:
  7.2 0.0 all-gather.6.cloned.1.call-start
  7.2 0.7 all-gather.6.cloned.1.call-update
  7.9 0.0 all-gather.8.cloned.1.call-start
  8.0 0.7 all-gather.8.cloned.1.call-update
  8.7 0.0 all-gather.4.cloned.1.call-start
  8.7 0.7 all-gather.4.cloned.1.call-update
  9.5 1.2 reduce-window.6
  10.7 0.1 slice.18
  10.8 0.1 copy.23
  10.9 0.1 copy.24
  11.0 0.1 add_bitcast_fusion
  11.2 1.2 scatter_custom_fusion
  12.4 0.0 copy-start.3
  12.4 2.6 gather_fusion.1
  15.0 4.4 %all-to-all-start.1 = ((bf16[4,72,896]{2,1,0:T(8,128)(2,1)}), bf16[4,72,896]{2,1,0:T(8,128)(2,1)S(1)}, u32[]{:S(2)}, u32[]{:S(2)}) async-start(bf16[4,72,896]{2,1,0:T(8,128)(2,1)} %bitcast.8), calls=%async_computation.1 | async-start | bytes 1032192 | tf_op jit(solution)/shard_map/all_to_all | solution.py:40
  19.4 0.1 multiply_convert_fusion.1
  19.6 2.6 gather_fusion
  22.2 6.0 %all-to-all-done.1 = bf16[4,72,896]{2,1,0:T(8,128)(2,1)S(1)} async-done(((bf16[4,72,896]{2,1,0:T(8,128)(2,1)}), bf16[4,72,896]{2,1,0:T(8,128)(2,1)S(1)}, u32[]{:S(2)}, u32[]{:S(2)}) %all-to-all-start.1) | async-done | bytes 516128 | tf_op jit(solution)/shard_map/all_to_all | solution.py:40
  28.1 3.5 %all-to-all-start = ((bf16[4,72,896]{2,1,0:T(8,128)(2,1)}), bf16[4,72,896]{2,1,0:T(8,128)(2,1)S(1)}, u32[]{:S(2)}, u32[]{:S(2)}) async-start(bf16[4,72,896]{2,1,0:T(8,128)(2,1)} %bitcast.5), calls=%async_computation | async-start | bytes 1032192 | tf_op jit(solution)/shard_map/all_to_all | solution.py:59
  31.6 0.0 all-reduce.6.cloned.1.call-start
  31.7 10.8 %all-gather.6.cloned.1.call-done = bf16[1,896,1024]{2,1,0:T(8,128)(2,1)} async-done(((bf16[1,896,512]{2,1,0:T(8,128)(2,1)}), bf16[1,896,1024]{2,1,0:T(8,128)(2,1)}) %all-gather.6.cloned.1.call-update) | async-done | bytes 1835024 | tf_op jit(solution)/shard_map/all_gather | solution.py:44
  42.4 3.1 fusion.16
  45.5 28.6 %all-gather.8.cloned.1.call-done = bf16[1,896,1024]{2,1,0:T(8,128)(2,1)} async-done(((bf16[1,896,512]{2,1,0:T(8,128)(2,1)}), bf16[1,896,1024]{2,1,0:T(8,128)(2,1)}) %all-gather.8.cloned.1.call-update) | async-done | bytes 1835024 | tf_op jit(solution)/shard_map/all_gather | solution.py:43
  74.1 3.1 fusion.19
  77.2 0.0 all-to-all-done
  77.2 28.6 %all-gather.4.cloned.1.call-done = bf16[1,1024,896]{2,1,0:T(8,128)(2,1)} async-done(((bf16[1,512,896]{2,1,0:T(8,128)(2,1)}), bf16[1,1024,896]{2,1,0:T(8,128)(2,1)}) %all-gather.4.cloned.1.call-update) | async-done | bytes 1835024 | tf_op jit(solution)/shard_map/all_gather | solution.py:45
  105.9 3.3 %fusion.13 = bf16[288,1024]{1,0:T(8,128)(2,1)} fusion(bf16[288,896]{1,0:T(8,128)(2,1)S(1)} %bitcast.80, bf16[1,1024,896]{2,1,0:T(8,128)(2,1)} %all-gather.4.cloned.1.call-done), kind=kOutput, calls=%fused_computation.24 | convolution fusion | flops 528777216 | bytes 2940928 | tf_op jit(solution)/shard_map/dot_general | solution.py:8
  109.1 0.0 all-reduce.6.cloned.1.call-update
  109.2 75.7 %all-reduce.6.cloned.1.call-done = (bf16[288,1024]{1,0:T(8,128)(2,1)}, bf16[288,1024]{1,0:T(8,128)(2,1)}, bf16[288,1024]{1,0:T(8,128)(2,1)}) async-done(((bf16[288,1024]{1,0:T(8,128)(2,1)}, bf16[288,1024]{1,0:T(8,128)(2,1)}, bf16[288,1024]{1,0:T(8,128)(2,1)}), (bf16[288,1024]{1,0:T(8,128)(2,1)}, bf16[288,1024]{1,0:T(8,128)(2,1)}, bf16[288,1024]{1,0:T(8,128)(2,1)})) %all-reduce.6.cloned.1.call-update) | async-done | bytes 1769488 | tf_op jit(solution)/shard_map/psum | solution.py:54
  184.9 2.6 fusion
  187.6 1.7 fusion.22
  189.3 3.5 %all-to-all-start.2 = ((bf16[4,72,896]{2,1,0:T(8,128)(2,1)}), bf16[4,72,896]{2,1,0:T(8,128)(2,1)S(1)}, u32[]{:S(2)}, u32[]{:S(2)}) async-start(bf16[4,72,896]{2,1,0:T(8,128)(2,1)} %bitcast.12), calls=%async_computation.2 | async-start | bytes 1032192 | tf_op jit(solution)/shard_map/all_to_all | solution.py:66
  192.8 2.8 convert_bitcast_fusion.2
  195.5 6.6 %copy.25 = bf16[1,896,1024]{1,0,2:T(2,128)(2,1)} copy(bf16[1,896,1024]{2,1,0:T(8,128)(2,1)S(1)} %convert_bitcast_fusion.2) | data formatting | bytes 3670016 | tf_op jit(solution)/shard_map/broadcast_in_dim | solution.py:75
  202.2 0.5 broadcast.68
  202.7 12.1 %reduce.9 = bf16[1024,896]{1,0:T(8,128)(2,1)S(1)} reduce(bf16[1024,1,896]{2,1,0:T(2,128)(2,1)} %bitcast.68, bf16[]{:T(256)} %broadcast.68), dimensions={1}, to_apply=%bitcast.51.reduce_sub_computation | reduce | bytes 3670018
  214.8 1.5 reshape.120
  216.3 0.0 all-to-all-done.2
  216.3 4.9 %all-to-all-start.3 = ((bf16[2,2,229376]{2,1,0:T(2,128)(2,1)}), bf16[2,2,229376]{2,1,0:T(2,128)(2,1)}, u32[]{:S(2)}, u32[]{:S(2)}) async-start(bf16[2,2,229376]{2,1,0:T(2,128)(2,1)} %reshape.120), calls=%async_computation.3 | async-start | bytes 3670016 | tf_op jit(solution)/shard_map/all_to_all | solution.py:79
  221.2 2.5 convert_bitcast_fusion.1
  223.7 6.6 %copy.26 = bf16[1,896,1024]{1,0,2:T(2,128)(2,1)} copy(bf16[1,896,1024]{2,1,0:T(8,128)(2,1)S(1)} %convert_bitcast_fusion.1) | data formatting | bytes 3670016 | tf_op jit(solution)/shard_map/broadcast_in_dim | solution.py:76
  230.4 12.1 %reduce.10 = bf16[1024,896]{1,0:T(8,128)(2,1)S(1)} reduce(bf16[1024,1,896]{2,1,0:T(2,128)(2,1)} %bitcast.70, bf16[]{:T(256)} %broadcast.68), dimensions={1}, to_apply=%bitcast.53.reduce_sub_computation | reduce | bytes 3670018
  242.5 1.5 reshape.122
  244.0 0.1 all-to-all-done.3
  244.0 4.8 %all-to-all-start.4 = ((bf16[2,2,229376]{2,1,0:T(2,128)(2,1)}), bf16[2,2,229376]{2,1,0:T(2,128)(2,1)}, u32[]{:S(2)}, u32[]{:S(2)}) async-start(bf16[2,2,229376]{2,1,0:T(2,128)(2,1)} %reshape.122), calls=%async_computation.4 | async-start | bytes 3670016 | tf_op jit(solution)/shard_map/all_to_all | solution.py:80
  248.9 1.4 convert_bitcast_fusion
  250.3 4.6 %copy.37 = bf16[1,1024,896]{2,0,1:T(2,128)(2,1)} copy(bf16[1,1024,896]{2,1,0:T(8,128)(2,1)S(1)} %convert_bitcast_fusion) | data formatting | bytes 3670016 | tf_op jit(solution)/shard_map/broadcast_in_dim | solution.py:77
  254.9 12.1 %reduce.11 = bf16[1024,896]{1,0:T(8,128)(2,1)S(1)} reduce(bf16[1024,1,896]{2,1,0:T(2,128)(2,1)} %bitcast.69, bf16[]{:T(256)} %broadcast.68), dimensions={1}, to_apply=%bitcast.66.reduce_sub_computation | reduce | bytes 3670018
  267.0 1.6 reshape.124
  268.6 3.3 %all-to-all-done.4 = bf16[2,2,229376]{2,1,0:T(2,128)(2,1)} async-done(((bf16[2,2,229376]{2,1,0:T(2,128)(2,1)}), bf16[2,2,229376]{2,1,0:T(2,128)(2,1)}, u32[]{:S(2)}, u32[]{:S(2)}) %all-to-all-start.4) | async-done | bytes 1835040 | tf_op jit(solution)/shard_map/all_to_all | solution.py:80
  271.8 3.9 %all-to-all-start.5 = ((bf16[2,2,229376]{2,1,0:T(2,128)(2,1)}), bf16[2,2,229376]{2,1,0:T(2,128)(2,1)S(1)}, u32[]{:S(2)}, u32[]{:S(2)}) async-start(bf16[2,2,229376]{2,1,0:T(2,128)(2,1)} %reshape.124), calls=%async_computation.5 | async-start | bytes 3670016 | tf_op jit(solution)/shard_map/all_to_all | solution.py:82
  275.8 1.0 gather_fusion.2
  276.8 0.9 multiply_convert_fusion
  277.7 4.0 %reshape.121 = bf16[1024,1,896]{2,1,0:T(2,128)(2,1)} reshape(bf16[2,2,229376]{2,1,0:T(2,128)(2,1)} %all-to-all-done.3) | data formatting | bytes 3670016
  281.7 3.6 %copy.30 = bf16[1,896,1024]{1,2,0:T(8,128)(2,1)} copy(bf16[1,896,1024]{1,0,2:T(2,128)(2,1)} %bitcast.71) | data formatting | bytes 3670016
  285.2 2.3 reduce_sum.46
  287.5 1.3 copy.28
  288.8 4.0 %reshape.123 = bf16[1024,1,896]{2,1,0:T(2,128)(2,1)} reshape(bf16[2,2,229376]{2,1,0:T(2,128)(2,1)} %all-to-all-done.4) | data formatting | bytes 3670016
  292.8 3.6 %copy.31 = bf16[1,896,1024]{1,2,0:T(8,128)(2,1)} copy(bf16[1,896,1024]{1,0,2:T(2,128)(2,1)} %bitcast.72) | data formatting | bytes 3670016
  296.3 2.3 reduce_sum.47
  298.7 1.3 copy.29
  300.0 2.8 reshape.125
  302.7 2.3 copy.32
  305.1 1.5 reduce.8
  (34 shorter events, 0.2 us)
Async XLA Ops:
  7.2 2.2 copy-start.2
  7.2 35.2 %all-gather.6.cloned.1.call-start = ((), (), s32[]{:S(2)}) async-start(), calls=%async_computation.7 | async-start | bytes 2752512 | tf_op jit(solution)/shard_map/all_gather | solution.py:44
  7.9 3.2 %copy-start = (bf16[192,896]{1,0:T(8,128)(2,1)S(1)}, bf16[192,896]{1,0:T(8,128)(2,1)}, u32[]{:S(2)}) copy-start(bf16[192,896]{1,0:T(8,128)(2,1)} %param.7) | copy-start | bytes 1032196
  7.9 66.2 %all-gather.8.cloned.1.call-start = ((), (), s32[]{:S(2)}) async-start(), calls=%async_computation.8 | async-start | bytes 2752512 | tf_op jit(solution)/shard_map/all_gather | solution.py:43
  8.7 97.2 %all-gather.4.cloned.1.call-start = ((), (), s32[]{:S(2)}) async-start(), calls=%async_computation.6 | async-start | bytes 2752512 | tf_op jit(solution)/shard_map/all_gather | solution.py:45
  12.4 7.0 %copy-start.3 = (f32[192]{0:T(256)S(1)}, f32[192]{0:T(256)}, u32[]{:S(2)}) copy-start(f32[192]{0:T(256)} %param.9) | copy-start | bytes 2308
  15.0 4.4 %copy-start.1 = (bf16[192,896]{1,0:T(8,128)(2,1)S(1)}, bf16[192,896]{1,0:T(8,128)(2,1)}, u32[]{:S(2)}) copy-start(bf16[192,896]{1,0:T(8,128)(2,1)} %param.8) | copy-start | bytes 1032196
  15.0 13.1 %all-to-all-start.1 = ((bf16[4,72,896]{2,1,0:T(8,128)(2,1)}), bf16[4,72,896]{2,1,0:T(8,128)(2,1)S(1)}, u32[]{:S(2)}, u32[]{:S(2)}) async-start(bf16[4,72,896]{2,1,0:T(8,128)(2,1)} %bitcast.8), calls=%async_computation.1 | async-start | bytes 1032192 | tf_op jit(solution)/shard_map/all_to_all | solution.py:40
  28.1 49.1 %all-to-all-start = ((bf16[4,72,896]{2,1,0:T(8,128)(2,1)}), bf16[4,72,896]{2,1,0:T(8,128)(2,1)S(1)}, u32[]{:S(2)}, u32[]{:S(2)}) async-start(bf16[4,72,896]{2,1,0:T(8,128)(2,1)} %bitcast.5), calls=%async_computation | async-start | bytes 1032192 | tf_op jit(solution)/shard_map/all_to_all | solution.py:59
  31.6 153.3 %all-reduce.6.cloned.1.call-start = ((), (), s32[]{:S(2)}) async-start(), calls=%async_computation.9 | async-start | bytes 3538944 | tf_op jit(solution)/shard_map/psum | solution.py:54
  105.9 79.0 %copy-start.5 = (bf16[1,896,1024]{2,1,0:T(8,128)(2,1)S(1)}, bf16[1,896,1024]{2,1,0:T(8,128)(2,1)}, u32[]{:S(2)}) copy-start(bf16[1,896,1024]{2,1,0:T(8,128)(2,1)} %all-gather.8.cloned.1.call-done) | copy-start | bytes 5505028
  184.9 2.7 copy-start.4
  184.9 2.7 copy-start.7
  184.9 2.7 copy-start.9
  189.3 27.0 %all-to-all-start.2 = ((bf16[4,72,896]{2,1,0:T(8,128)(2,1)}), bf16[4,72,896]{2,1,0:T(8,128)(2,1)S(1)}, u32[]{:S(2)}, u32[]{:S(2)}) async-start(bf16[4,72,896]{2,1,0:T(8,128)(2,1)} %bitcast.12), calls=%async_computation.2 | async-start | bytes 1032192 | tf_op jit(solution)/shard_map/all_to_all | solution.py:66
  216.3 27.7 %all-to-all-start.3 = ((bf16[2,2,229376]{2,1,0:T(2,128)(2,1)}), bf16[2,2,229376]{2,1,0:T(2,128)(2,1)}, u32[]{:S(2)}, u32[]{:S(2)}) async-start(bf16[2,2,229376]{2,1,0:T(2,128)(2,1)} %reshape.120), calls=%async_computation.3 | async-start | bytes 3670016 | tf_op jit(solution)/shard_map/all_to_all | solution.py:79
  244.0 4.9 %copy-start.6 = (bf16[288,1024]{1,0:T(8,128)(2,1)S(1)}, bf16[288,1024]{1,0:T(8,128)(2,1)}, u32[]{:S(2)}) copy-start(bf16[288,1024]{1,0:T(8,128)(2,1)} %get-tuple-element.8) | copy-start | bytes 1769476
  244.0 4.9 %copy-start.8 = (bf16[288,1024]{1,0:T(8,128)(2,1)S(1)}, bf16[288,1024]{1,0:T(8,128)(2,1)}, u32[]{:S(2)}) copy-start(bf16[288,1024]{1,0:T(8,128)(2,1)} %get-tuple-element.10) | copy-start | bytes 1769476
  244.0 27.8 %all-to-all-start.4 = ((bf16[2,2,229376]{2,1,0:T(2,128)(2,1)}), bf16[2,2,229376]{2,1,0:T(2,128)(2,1)}, u32[]{:S(2)}, u32[]{:S(2)}) async-start(bf16[2,2,229376]{2,1,0:T(2,128)(2,1)} %reshape.122), calls=%async_computation.4 | async-start | bytes 3670016 | tf_op jit(solution)/shard_map/all_to_all | solution.py:80
  271.8 28.1 %all-to-all-start.5 = ((bf16[2,2,229376]{2,1,0:T(2,128)(2,1)}), bf16[2,2,229376]{2,1,0:T(2,128)(2,1)S(1)}, u32[]{:S(2)}, u32[]{:S(2)}) async-start(bf16[2,2,229376]{2,1,0:T(2,128)(2,1)} %reshape.124), calls=%async_computation.5 | async-start | bytes 3670016 | tf_op jit(solution)/shard_map/all_to_all | solution.py:82
Sparse Core Ops, SparseCore 0:
  9.5 32.8 all-gather.5
  44.0 30.1 all-gather.7
  75.7 30.1 all-gather.3
  109.3 75.5 all-reduce.5
where the time goes:
time: 314 us; the launch traced here: 313 us
  waiting for transfers between devices  155 us (49%)
  local copies, waits for them, and re-layouts  53.5 us (17%)
  other arithmetic  44.8 us (14%)
  starting transfers between devices  25.1 us (8%)
  matrix products  20.5 us (7%)
  between operations  14 us (4%)
    psum x1, waiting for transfers between devices, local(): lax.psum(part_up.astype(jnp.bfloat16), 'seq').astype(jnp.float32)  75.7 us
    unnamed x4, other arithmetic  36.3 us
    all_gather x1, waiting for transfers between devices, local(): lax.all_gather(down_weight, 'replica', axis=1, tiled=True)  28.6 us
    all_gather x1, waiting for transfers between devices, local(): lax.all_gather(gate_weight, 'replica', axis=2, tiled=True)  28.6 us
    unnamed x33, local copies, waits for them, and re-layouts  27.9 us
    all_gather x1, waiting for transfers between devices, local(): lax.all_gather(up_weight, 'replica', axis=2, tiled=True)  10.8 us
    dot_general x3, matrix products, matmul_last(): lax.dot_general(left, right, (((1,), (1,)), ((), ())), preferred_element_...  7.66 us
    broadcast_in_dim x1, local copies, waits for them, and re-layouts, local(): grad_gate = matmul_first(rows_x, gate_delta).astype(jnp.bfloat16)[None]  6.63 us
  transfers between devices with their start and end apart: 10, of which 7 were waited for; matrix products, arithmetic and copies ran while one was open for 33% of the time, Pallas kernels for 0%

commit v1 on v0

--- a/solution.py
+++ b/solution.py
@@ -51,7 +51,7 @@
     part_up = jnp.dot(rows_x, w_up, preferred_element_type=jnp.float32)
     gate, upper = (
         lax.psum(part_gate.astype(jnp.bfloat16), "seq").astype(jnp.float32),
-        lax.psum(part_up.astype(jnp.bfloat16), "seq").astype(jnp.float32),
+        jnp.sum(lax.all_gather(part_up.astype(jnp.bfloat16), "seq"), axis=0).astype(jnp.float32),
     )
     sigma = jax.nn.sigmoid(gate)
     active = gate * sigma

time: 314 us -> 321 us (1.022)
  waiting for transfers between devices: 155 us -> 163 us
    all_gather x0 -> x1, waiting for transfers between devices: none -> 24.4 us  [local(): lax.all_gather(part_up.astype(jnp.bfloat16), 'seq')]
    psum x1, waiting for transfers between devices: 75.7 us -> 55.8 us  [local(): hgrad = lax.psum(part_dh.astype(jnp.bfloat16), 'seq').astype(jnp.float32)]
    all_gather x1, waiting for transfers between devices: 28.6 us -> 10.7 us  [local(): lax.all_gather(down_weight, 'replica', axis=1, tiled=True)]
    all_gather x1, waiting for transfers between devices: 10.8 us -> 28.6 us  [local(): lax.all_gather(up_weight, 'replica', axis=2, tiled=True)]
    all_to_all x1, waiting for transfers between devices: 0.01 us -> 6.1 us  [local(): lax.all_to_all(send_g, 'expert', split_axis=0, concat_axis=0, tiled=True)]
    all_to_all x1, waiting for transfers between devices: 5.96 us -> 0.01 us  [local(): lax.all_to_all(send_x, 'expert', split_axis=0, concat_axis=0, tiled=True)]
    all_to_all x1, waiting for transfers between devices: 0.01 us -> 4.01 us  [local(): lax.all_to_all(grad_down, 'replica', split_axis=1, concat_axis=0, tiled=T...]
    all_to_all x1, waiting for transfers between devices: 3.28 us -> 0.01 us  [local(): lax.all_to_all(grad_up, 'replica', split_axis=2, concat_axis=0, tiled=True)]
  transfers between devices with their start and end apart: 10 -> 11, of which waited for: 7 -> 8; matrix products, arithmetic and copies ran while one was open for 33% -> 34% of each run, Pallas kernels for 0% -> 0%
where the time goes in v1:
time: 321 us; the launch traced here: 320 us
  waiting for transfers between devices  163 us (51%)
  local copies, waits for them, and re-layouts  52.3 us (16%)
  other arithmetic  44.1 us (14%)
  starting transfers between devices  25.2 us (8%)
  matrix products  20.8 us (6%)
  between operations  14.1 us (4%)
    psum x1, waiting for transfers between devices, local(): hgrad = lax.psum(part_dh.astype(jnp.bfloat16), 'seq').astype(jnp.float32)  55.8 us
    unnamed x4, other arithmetic  36.3 us
    all_gather x1, waiting for transfers between devices, local(): lax.all_gather(gate_weight, 'replica', axis=2, tiled=True)  28.6 us
    all_gather x1, waiting for transfers between devices, local(): lax.all_gather(up_weight, 'replica', axis=2, tiled=True)  28.6 us
    unnamed x35, local copies, waits for them, and re-layouts  26.7 us
    all_gather x1, waiting for transfers between devices, local(): lax.all_gather(part_up.astype(jnp.bfloat16), 'seq')  24.4 us
    all_gather x1, waiting for transfers between devices, local(): lax.all_gather(down_weight, 'replica', axis=1, tiled=True)  10.7 us
    dot_general x3, matrix products, matmul_last(): lax.dot_general(left, right, (((1,), (1,)), ((), ())), preferred_element_...  7.97 us
  transfers between devices with their start and end apart: 11, of which 8 were waited for; matrix products, arithmetic and copies ran while one was open for 34% of the time, Pallas kernels for 0%

profile of v1, /device:TPU:0, one launch (start us, length us, event | category | flops | bytes accessed | tf_op | source)
XLA Modules:
  0.0 320.0 jit_solution(4392914632054318229)
XLA Ops:
  7.2 0.0 all-gather.6.cloned.1.call-start
  7.2 0.7 all-gather.6.cloned.1.call-update
  7.9 0.0 all-gather.10.cloned.1.call-start
  8.0 0.7 all-gather.10.cloned.1.call-update
  8.7 0.0 all-gather.8.cloned.1.call-start
  8.7 0.7 all-gather.8.cloned.1.call-update
  9.5 1.2 reduce-window.6
  10.7 0.1 slice.18
  10.8 0.1 copy.23
  10.9 0.1 copy.24
  11.0 0.1 multiply_convert_fusion.1
  11.1 0.1 add_bitcast_fusion
  11.3 1.2 scatter_custom_fusion
  12.5 2.6 gather_fusion
  15.1 4.4 %all-to-all-start = ((bf16[4,72,896]{2,1,0:T(8,128)(2,1)}), bf16[4,72,896]{2,1,0:T(8,128)(2,1)S(1)}, u32[]{:S(2)}, u32[]{:S(2)}) async-start(bf16[4,72,896]{2,1,0:T(8,128)(2,1)} %bitcast.5), calls=%async_computation | async-start | bytes 1032192 | tf_op jit(solution)/shard_map/all_to_all | solution.py:59
  19.6 2.6 gather_fusion.1
  22.2 6.1 %all-to-all-done = bf16[4,72,896]{2,1,0:T(8,128)(2,1)S(1)} async-done(((bf16[4,72,896]{2,1,0:T(8,128)(2,1)}), bf16[4,72,896]{2,1,0:T(8,128)(2,1)S(1)}, u32[]{:S(2)}, u32[]{:S(2)}) %all-to-all-start) | async-done | bytes 516128 | tf_op jit(solution)/shard_map/all_to_all | solution.py:59
  28.3 3.5 %all-to-all-start.1 = ((bf16[4,72,896]{2,1,0:T(8,128)(2,1)}), bf16[4,72,896]{2,1,0:T(8,128)(2,1)S(1)}, u32[]{:S(2)}, u32[]{:S(2)}) async-start(bf16[4,72,896]{2,1,0:T(8,128)(2,1)} %bitcast.8), calls=%async_computation.1 | async-start | bytes 1032192 | tf_op jit(solution)/shard_map/all_to_all | solution.py:40
  31.7 0.0 all-reduce.6.cloned.1.call-start
  31.8 10.7 %all-gather.6.cloned.1.call-done = bf16[1,1024,896]{2,1,0:T(8,128)(2,1)} async-done(((bf16[1,512,896]{2,1,0:T(8,128)(2,1)}), bf16[1,1024,896]{2,1,0:T(8,128)(2,1)}) %all-gather.6.cloned.1.call-update) | async-done | bytes 1835024 | tf_op jit(solution)/shard_map/all_gather | solution.py:45
  42.4 3.1 fusion.13
  45.6 28.6 %all-gather.10.cloned.1.call-done = bf16[1,896,1024]{2,1,0:T(8,128)(2,1)} async-done(((bf16[1,896,512]{2,1,0:T(8,128)(2,1)}), bf16[1,896,1024]{2,1,0:T(8,128)(2,1)}) %all-gather.10.cloned.1.call-update) | async-done | bytes 1835024 | tf_op jit(solution)/shard_map/all_gather | solution.py:43
  74.2 3.1 fusion.19
  77.3 0.0 all-gather.12.cloned.1.call-start
  77.3 28.6 %all-gather.8.cloned.1.call-done = bf16[1,896,1024]{2,1,0:T(8,128)(2,1)} async-done(((bf16[1,896,512]{2,1,0:T(8,128)(2,1)}), bf16[1,896,1024]{2,1,0:T(8,128)(2,1)}) %all-gather.8.cloned.1.call-update) | async-done | bytes 1835024 | tf_op jit(solution)/shard_map/all_gather | solution.py:44
  105.9 3.1 fusion.16
  109.0 55.8 %all-reduce.6.cloned.1.call-done = (bf16[288,1024]{1,0:T(8,128)(2,1)}, bf16[288,1024]{1,0:T(8,128)(2,1)}) async-done(((bf16[288,1024]{1,0:T(8,128)(2,1)}, bf16[288,1024]{1,0:T(8,128)(2,1)}), (bf16[288,1024]{1,0:T(8,128)(2,1)}, bf16[288,1024]{1,0:T(8,128)(2,1)})) %all-reduce.6.cloned.1.call-update) | async-done | bytes 1179664 | tf_op jit(solution)/shard_map/psum | solution.py:62
  164.8 2.5 convert_bitcast_fusion.1
  167.3 6.6 %copy.26 = bf16[1,896,1024]{1,0,2:T(2,128)(2,1)} copy(bf16[1,896,1024]{2,1,0:T(8,128)(2,1)S(1)} %convert_bitcast_fusion.1) | data formatting | bytes 3670016 | tf_op jit(solution)/shard_map/broadcast_in_dim | solution.py:76
  174.0 0.5 broadcast.68
  174.5 12.1 %reduce.11 = bf16[1024,896]{1,0:T(8,128)(2,1)S(1)} reduce(bf16[1024,1,896]{2,1,0:T(2,128)(2,1)} %bitcast.69, bf16[]{:T(256)} %broadcast.68), dimensions={1}, to_apply=%bitcast.54.reduce_sub_computation | reduce | bytes 3670018
  186.6 1.5 reshape.123
  188.1 3.7 %all-to-all-start.4 = ((bf16[2,2,229376]{2,1,0:T(2,128)(2,1)}), bf16[2,2,229376]{2,1,0:T(2,128)(2,1)S(1)}, u32[]{:S(2)}, u32[]{:S(2)}) async-start(bf16[2,2,229376]{2,1,0:T(2,128)(2,1)} %reshape.123), calls=%async_computation.4 | async-start | bytes 3670016 | tf_op jit(solution)/shard_map/all_to_all | solution.py:80
  191.8 24.4 %all-gather.12.cloned.1.call-done = bf16[1152,1024]{1,0:T(8,128)(2,1)} async-done(((bf16[288,1024]{1,0:T(8,128)(2,1)}), bf16[1152,1024]{1,0:T(8,128)(2,1)}) %all-gather.12.cloned.1.call-update) | async-done | bytes 2359312 | tf_op jit(solution)/shard_map/all_gather | solution.py:54
  216.2 2.2 reduce_sum.58
  218.4 3.1 fusion
  221.5 1.7 fusion.22
  223.3 1.2 copy-done
  224.5 3.7 %all-to-all-start.2 = ((bf16[4,72,896]{2,1,0:T(8,128)(2,1)}), bf16[4,72,896]{2,1,0:T(8,128)(2,1)S(1)}, u32[]{:S(2)}, u32[]{:S(2)}) async-start(bf16[4,72,896]{2,1,0:T(8,128)(2,1)} %bitcast.13), calls=%async_computation.2 | async-start | bytes 1032192 | tf_op jit(solution)/shard_map/all_to_all | solution.py:66
  228.2 2.8 convert_bitcast_fusion.2
  230.9 6.6 %copy.25 = bf16[1,896,1024]{1,0,2:T(2,128)(2,1)} copy(bf16[1,896,1024]{2,1,0:T(8,128)(2,1)S(1)} %convert_bitcast_fusion.2) | data formatting | bytes 3670016 | tf_op jit(solution)/shard_map/broadcast_in_dim | solution.py:75
  237.6 12.1 %reduce.10 = bf16[1024,896]{1,0:T(8,128)(2,1)S(1)} reduce(bf16[1024,1,896]{2,1,0:T(2,128)(2,1)} %bitcast.71, bf16[]{:T(256)} %broadcast.68), dimensions={1}, to_apply=%bitcast.52.reduce_sub_computation | reduce | bytes 3670018
  249.7 1.6 reshape.121
  251.2 4.8 %all-to-all-start.3 = ((bf16[2,2,229376]{2,1,0:T(2,128)(2,1)}), bf16[2,2,229376]{2,1,0:T(2,128)(2,1)}, u32[]{:S(2)}, u32[]{:S(2)}) async-start(bf16[2,2,229376]{2,1,0:T(2,128)(2,1)} %reshape.121), calls=%async_computation.3 | async-start | bytes 3670016 | tf_op jit(solution)/shard_map/all_to_all | solution.py:79
  256.1 1.4 convert_bitcast_fusion
  257.5 4.6 %copy.37 = bf16[1,1024,896]{2,0,1:T(2,128)(2,1)} copy(bf16[1,1024,896]{2,1,0:T(8,128)(2,1)S(1)} %convert_bitcast_fusion) | data formatting | bytes 3670016 | tf_op jit(solution)/shard_map/broadcast_in_dim | solution.py:77
  262.1 12.1 %reduce.12 = bf16[1024,896]{1,0:T(8,128)(2,1)S(1)} reduce(bf16[1024,1,896]{2,1,0:T(2,128)(2,1)} %bitcast.70, bf16[]{:T(256)} %broadcast.68), dimensions={1}, to_apply=%bitcast.67.reduce_sub_computation | reduce | bytes 3670018
  274.2 1.5 reshape.125
  275.7 3.3 %all-to-all-done.3 = bf16[2,2,229376]{2,1,0:T(2,128)(2,1)} async-done(((bf16[2,2,229376]{2,1,0:T(2,128)(2,1)}), bf16[2,2,229376]{2,1,0:T(2,128)(2,1)}, u32[]{:S(2)}, u32[]{:S(2)}) %all-to-all-start.3) | async-done | bytes 1835040 | tf_op jit(solution)/shard_map/all_to_all | solution.py:79
  278.9 4.9 %all-to-all-start.5 = ((bf16[2,2,229376]{2,1,0:T(2,128)(2,1)}), bf16[2,2,229376]{2,1,0:T(2,128)(2,1)}, u32[]{:S(2)}, u32[]{:S(2)}) async-start(bf16[2,2,229376]{2,1,0:T(2,128)(2,1)} %reshape.125), calls=%async_computation.5 | async-start | bytes 3670016 | tf_op jit(solution)/shard_map/all_to_all | solution.py:82
  283.9 2.8 reshape.124
  286.7 2.3 copy.31
  289.0 0.9 reduce_sum.60
  289.9 1.3 copy.29
  291.2 1.0 gather_fusion.2
  292.3 0.9 multiply_convert_fusion
  293.1 4.0 %reshape.122 = bf16[1024,1,896]{2,1,0:T(2,128)(2,1)} reshape(bf16[2,2,229376]{2,1,0:T(2,128)(2,1)} %all-to-all-done.3) | data formatting | bytes 3670016
  297.1 2.3 copy.30
  299.4 0.9 reduce_sum.59
  300.3 1.3 copy.28
  301.6 4.0 %all-to-all-done.5 = bf16[2,2,229376]{2,1,0:T(2,128)(2,1)} async-done(((bf16[2,2,229376]{2,1,0:T(2,128)(2,1)}), bf16[2,2,229376]{2,1,0:T(2,128)(2,1)}, u32[]{:S(2)}, u32[]{:S(2)}) %all-to-all-start.5) | async-done | bytes 1835040 | tf_op jit(solution)/shard_map/all_to_all | solution.py:82
  305.6 4.0 %reshape.126 = bf16[1024,1,896]{2,1,0:T(2,128)(2,1)} reshape(bf16[2,2,229376]{2,1,0:T(2,128)(2,1)} %all-to-all-done.5) | data formatting | bytes 3670016
  309.6 2.3 copy.32
  311.9 1.5 reduce.9
  (40 shorter events, 0.3 us)
Async XLA Ops:
  7.2 2.3 copy-start.5
  7.2 3.8 %copy-start.3 = (bf16[192,896]{1,0:T(8,128)(2,1)S(1)}, bf16[192,896]{1,0:T(8,128)(2,1)}, u32[]{:S(2)}) copy-start(bf16[192,896]{1,0:T(8,128)(2,1)} %param.8) | copy-start | bytes 1032196
  7.2 3.8 %copy-start.6 = (f32[192]{0:T(256)S(1)}, f32[192]{0:T(256)}, u32[]{:S(2)}) copy-start(f32[192]{0:T(256)} %param.9) | copy-start | bytes 2308
  7.2 35.2 %all-gather.6.cloned.1.call-start = ((), (), s32[]{:S(2)}) async-start(), calls=%async_computation.6 | async-start | bytes 2752512 | tf_op jit(solution)/shard_map/all_gather | solution.py:45
  7.9 66.2 %all-gather.10.cloned.1.call-start = ((), (), s32[]{:S(2)}) async-start(), calls=%async_computation.8 | async-start | bytes 2752512 | tf_op jit(solution)/shard_map/all_gather | solution.py:43
  8.7 97.2 %all-gather.8.cloned.1.call-start = ((), (), s32[]{:S(2)}) async-start(), calls=%async_computation.7 | async-start | bytes 2752512 | tf_op jit(solution)/shard_map/all_gather | solution.py:44
  15.1 4.4 %copy-start.4 = (bf16[192,896]{1,0:T(8,128)(2,1)S(1)}, bf16[192,896]{1,0:T(8,128)(2,1)}, u32[]{:S(2)}) copy-start(bf16[192,896]{1,0:T(8,128)(2,1)} %param.7) | copy-start | bytes 1032196
  15.1 13.1 %all-to-all-start = ((bf16[4,72,896]{2,1,0:T(8,128)(2,1)}), bf16[4,72,896]{2,1,0:T(8,128)(2,1)S(1)}, u32[]{:S(2)}, u32[]{:S(2)}) async-start(bf16[4,72,896]{2,1,0:T(8,128)(2,1)} %bitcast.5), calls=%async_computation | async-start | bytes 1032192 | tf_op jit(solution)/shard_map/all_to_all | solution.py:59
  28.3 17.3 %all-to-all-start.1 = ((bf16[4,72,896]{2,1,0:T(8,128)(2,1)}), bf16[4,72,896]{2,1,0:T(8,128)(2,1)S(1)}, u32[]{:S(2)}, u32[]{:S(2)}) async-start(bf16[4,72,896]{2,1,0:T(8,128)(2,1)} %bitcast.8), calls=%async_computation.1 | async-start | bytes 1032192 | tf_op jit(solution)/shard_map/all_to_all | solution.py:40
  31.7 133.1 %all-reduce.6.cloned.1.call-start = ((), (), s32[]{:S(2)}) async-start(), calls=%async_computation.10 | async-start | bytes 2359296 | tf_op jit(solution)/shard_map/psum | solution.py:62
  45.6 119.2 %copy-start.2 = (bf16[4,72,896]{2,1,0:T(8,128)(2,1)}, bf16[4,72,896]{2,1,0:T(8,128)(2,1)S(1)}, u32[]{:S(2)}) copy-start(bf16[4,72,896]{2,1,0:T(8,128)(2,1)S(1)} %all-to-all-done.1) | copy-start | bytes 1548292
  77.3 138.9 %all-gather.12.cloned.1.call-start = ((), (), s32[]{:S(2)}) async-start(), calls=%async_computation.9 | async-start | bytes 2949120 | tf_op jit(solution)/shard_map/all_gather | solution.py:54
  188.1 35.2 %all-to-all-start.4 = ((bf16[2,2,229376]{2,1,0:T(2,128)(2,1)}), bf16[2,2,229376]{2,1,0:T(2,128)(2,1)S(1)}, u32[]{:S(2)}, u32[]{:S(2)}) async-start(bf16[2,2,229376]{2,1,0:T(2,128)(2,1)} %reshape.123), calls=%async_computation.4 | async-start | bytes 3670016 | tf_op jit(solution)/shard_map/all_to_all | solution.py:80
  218.4 3.1 copy-start.7
  218.4 3.1 copy-start.8
  218.4 3.1 copy-start.10
  223.3 1.3 copy-start
  224.5 26.7 %all-to-all-start.2 = ((bf16[4,72,896]{2,1,0:T(8,128)(2,1)}), bf16[4,72,896]{2,1,0:T(8,128)(2,1)S(1)}, u32[]{:S(2)}, u32[]{:S(2)}) async-start(bf16[4,72,896]{2,1,0:T(8,128)(2,1)} %bitcast.13), calls=%async_computation.2 | async-start | bytes 1032192 | tf_op jit(solution)/shard_map/all_to_all | solution.py:66
  251.2 4.9 %copy-start.9 = (bf16[288,1024]{1,0:T(8,128)(2,1)S(1)}, bf16[288,1024]{1,0:T(8,128)(2,1)}, u32[]{:S(2)}) copy-start(bf16[288,1024]{1,0:T(8,128)(2,1)} %get-tuple-element.9) | copy-start | bytes 1769476
  251.2 27.7 %all-to-all-start.3 = ((bf16[2,2,229376]{2,1,0:T(2,128)(2,1)}), bf16[2,2,229376]{2,1,0:T(2,128)(2,1)}, u32[]{:S(2)}, u32[]{:S(2)}) async-start(bf16[2,2,229376]{2,1,0:T(2,128)(2,1)} %reshape.121), calls=%async_computation.3 | async-start | bytes 3670016 | tf_op jit(solution)/shard_map/all_to_all | solution.py:79
  275.7 8.2 %copy-start.1 = (bf16[2,2,229376]{2,1,0:T(2,128)(2,1)S(1)}, bf16[2,2,229376]{2,1,0:T(2,128)(2,1)}, u32[]{:S(2)}) copy-start(bf16[2,2,229376]{2,1,0:T(2,128)(2,1)} %copy-done) | copy-start | bytes 5505028
  278.9 26.7 %all-to-all-start.5 = ((bf16[2,2,229376]{2,1,0:T(2,128)(2,1)}), bf16[2,2,229376]{2,1,0:T(2,128)(2,1)}, u32[]{:S(2)}, u32[]{:S(2)}) async-start(bf16[2,2,229376]{2,1,0:T(2,128)(2,1)} %reshape.125), calls=%async_computation.5 | async-start | bytes 3670016 | tf_op jit(solution)/shard_map/all_to_all | solution.py:82
Sparse Core Ops, SparseCore 0:
  9.5 32.8 all-gather.5
  44.0 30.1 all-gather.9
  75.7 30.1 all-gather.7
  108.7 56.0 all-reduce.5
  166.8 49.3 all-gather.11
